TPU v7x, 32 devices: a whole 2x2x4 slice. The times are simulated.
32 devices in a mesh: seq: 8 (over y, x, core), head: 4 (over z).
Axes of the slice: x: 2, y: 2, z: 4, core: 2. Of those that a mesh axis runs over, the one named last changes fastest.
Arguments:
- out_grad: bfloat16 [2048, 4096], P('seq', 'head'), may hold values from -7.2 to 7.2
- x_in: bfloat16 [2048, 4096], P('seq', 'head'), may hold values from -6 to 6
- b_in: bfloat16 [2048, 128], P('seq'), may hold values from -2.5 to 2.5
- c_in: bfloat16 [2048, 128], P('seq'), may hold values from -2.5 to 2.5
- dt_raw: float32 [64, 2048], P('head', 'seq'), may hold values from -5.1 to -0.7
- dt_bias: float32 [64], P('head'), may hold values from -0.5 to 0.5
- a_log: float32 [64], P('head'), may hold values from -7.5 to 2.2
- d_skip: float32 [64], P('head'), may hold values from 0.5 to 1.5
- states: bfloat16 [8, 4096, 128], P('seq', 'head'), may hold values from -6 to 6
- w_out: bfloat16 [4096, 4096], P('head'), may hold values from -0.09375 to 0.09375
- w_in: bfloat16 [4096, 4096], P(None, 'head'), may hold values from -0.125 to 0.125
Outputs:
- in_grad: bfloat16 [4096, 2048], P('head', 'seq')
- bc_grad: bfloat16 [256, 2048], P('head', 'seq')
- dt_grad: float32 [64, 2048], P('head', 'seq')
- param_grad: float32 [3, 64], P(None, 'head')
All inputs are finite; a program needn't handle non-finite values.
Results may differ from a plain program's by a relative error of at most 0.015.
Values may be sent and summed in bfloat16 or wider, within the bound.
A program may use at most 64 MiB of HBM per device.

v0:
```python
import jax
import jax.numpy as jnp
from jax import lax
from jax.sharding import PartitionSpec as P


def entering(value, axis, join, neutral):
    count, mine = (lax.axis_size(axis), lax.axis_index(axis))
    pieces = jax.tree.map(lambda part: lax.all_gather(part, axis), value)
    pieces = jax.tree.map(lambda part: part[::-1], pieces)
    mine = count - 1 - mine
    so_far = jax.tree.map(
        lambda part, zero: jnp.full_like(part, 0) + jnp.asarray(zero, part.dtype), value, neutral
    )

    def turn(position, so_far):
        longer = join(so_far, jax.tree.map(lambda part: part[position], pieces))
        return jax.tree.map(lambda new, old: jnp.where(position < mine, new, old), longer, so_far)

    return lax.fori_loop(0, count - 1, turn, so_far)


def shards(out_grad, x_in, b_in, c_in, dt_raw, dt_bias, a_log, d_skip, states, w_out, w_in):
    tokens_here, inner_here = x_in.shape
    group_heads = dt_raw.shape[0]
    head_dim = inner_here // group_heads
    state_dim = b_in.shape[1]
    contract_last = (((1,), (1,)), ((), ()))
    head_sum = lax.dot_general(
        lax.all_gather(out_grad, "head", axis=1, tiled=True),
        w_out,
        contract_last,
        preferred_element_type=jnp.float32,
    )
    dy_heads = head_sum.astype(jnp.bfloat16).reshape(tokens_here, group_heads, head_dim)
    dy_wide = dy_heads.astype(jnp.float32)
    x_heads = x_in.reshape(tokens_here, group_heads, head_dim)
    x_wide = x_heads.astype(jnp.float32)
    decay_rate = jnp.exp(a_log)
    step_size = jax.nn.softplus(dt_raw + dt_bias[:, None])
    log_step = -decay_rate[:, None] * step_size
    cumlog = jnp.cumsum(log_step, axis=1)
    positions = jnp.arange(tokens_here)
    causal = positions[:, None] >= positions[None, :]
    log_gaps = cumlog[:, :, None] - cumlog[:, None, :]
    decay_mask = jnp.where(causal[None], jnp.exp(jnp.minimum(log_gaps, 0.0)), 0.0)
    scores = lax.dot_general(c_in, b_in, contract_last, preferred_element_type=jnp.float32)
    step_rows = step_size.T
    x_scaled = (x_wide * step_rows[:, :, None]).astype(jnp.bfloat16)
    pair_dots = jnp.einsum("ihp,jhp->hij", dy_heads, x_scaled, preferred_element_type=jnp.float32)
    kernel = (scores[None] * decay_mask).astype(jnp.bfloat16)
    intra_back = jnp.einsum("hij,ihp->jhp", kernel, dy_heads, preferred_element_type=jnp.float32)
    masked_dots = (pair_dots * decay_mask).astype(jnp.bfloat16)
    start_decay = jnp.exp(cumlog)
    dy_decay = (dy_wide * start_decay.T[:, :, None]).astype(jnp.bfloat16)
    local_state = jnp.einsum("ihp,in->hpn", dy_decay, c_in, preferred_element_type=jnp.float32)
    end_total = jnp.exp(cumlog[:, -1])
    entry_state = states.reshape(group_heads, head_dim, state_dim)
    db_intra = jnp.einsum("hij,in->nj", masked_dots, c_in, preferred_element_type=jnp.float32)
    dc_intra = jnp.einsum("hij,jn->ni", masked_dots, b_in, preferred_element_type=jnp.float32)
    dc_entry = jnp.einsum("ihp,hpn->ni", dy_decay, entry_state, preferred_element_type=jnp.float32)
    ystate = jnp.einsum("in,hpn->ihp", c_in, entry_state, preferred_element_type=jnp.float32)
    pair_weight = pair_dots * scores[None] * decay_mask
    state_terms = start_decay * jnp.sum(dy_wide * ystate, axis=2).T
    skip_terms = jnp.sum(dy_wide * x_wide, axis=(0, 2))

    def compose(earlier, nearer):
        return (nearer[0] * earlier[0], nearer[0][:, None, None] * earlier[1] + nearer[1])

    identity_pair = (jnp.ones_like(end_total), jnp.zeros_like(local_state))
    carried = entering((end_total, local_state), "seq", compose, identity_pair)[1]
    carried_bf = carried.astype(jnp.bfloat16)
    state_back = jnp.einsum("jn,hpn->jhp", b_in, carried_bf, preferred_element_type=jnp.float32)
    end_decay = jnp.exp(cumlog[:, -1:] - cumlog)
    end_weight = (step_size * end_decay).T
    x_grad = (
        (
            step_rows[:, :, None] * intra_back
            + end_weight[:, :, None] * state_back
            + d_skip[None, :, None] * dy_wide
        )
        .astype(jnp.bfloat16)
        .reshape(tokens_here, inner_here)
    )
    x_end = (x_wide * end_weight[:, :, None]).astype(jnp.bfloat16)
    db_entry = jnp.einsum("jhp,hpn->nj", x_end, carried_bf, preferred_element_type=jnp.float32)
    bc_part = jnp.concatenate([db_intra + db_entry, dc_intra + dc_entry], axis=0)
    end_terms = end_weight.T * jnp.sum(x_wide * state_back, axis=2).T
    cum_grad = pair_weight.sum(axis=2) - pair_weight.sum(axis=1) + state_terms - end_terms
    tail_grad = end_terms.sum(axis=1) + end_total * jnp.sum(
        entry_state.astype(jnp.float32) * carried, axis=(1, 2)
    )
    cum_grad = cum_grad.at[:, -1].add(tail_grad)
    step_grad = jnp.cumsum(cum_grad[:, ::-1], axis=1)[:, ::-1]
    dt_sum = (
        -decay_rate[:, None] * step_grad
        + jnp.sum(x_wide * (intra_back + end_decay.T[:, :, None] * state_back), axis=2).T
    )
    dt_grad = dt_sum * jax.nn.sigmoid(dt_raw + dt_bias[:, None])
    param_terms = jnp.stack(
        [jnp.sum(step_grad * log_step, axis=1), skip_terms, jnp.sum(dt_grad, axis=1)]
    )
    in_part = lax.psum_scatter(
        lax.dot_general(w_in, x_grad, contract_last, preferred_element_type=jnp.float32).astype(
            jnp.bfloat16
        ),
        "head",
        scatter_dimension=0,
        tiled=True,
    )
    bc_sum = lax.psum_scatter(bc_part.astype(jnp.bfloat16), "head", scatter_dimension=0, tiled=True)
    norm_scale = (lax.axis_size("seq") * tokens_here * head_dim) ** (-0.5)
    param_grad = lax.psum(param_terms, "seq") * norm_scale
    return (in_part, bc_sum, dt_grad, param_grad)


def solution(mesh):
    return jax.shard_map(
        shards,
        mesh=mesh,
        in_specs=(
            P("seq", "head"),
            P("seq", "head"),
            P("seq", None),
            P("seq", None),
            P("head", "seq"),
            P("head"),
            P("head"),
            P("head"),
            P("seq", "head", None),
            P("head", None),
            P(None, "head"),
        ),
        out_specs=(P("head", "seq"), P("head", "seq"), P("head", "seq"), P(None, "head")),
        check_vma=False,
    )
```

profile of v0, /device:TPU:0, one launch (start us, length us, event | category | flops | bytes accessed | tf_op | source)
XLA Modules:
  0.0 200.9 jit_solution(2288571976925971934)
XLA Ops:
  9.2 0.8 copy_bitcast_fusion.3
  11.0 1.4 fusion.35
  12.9 45.1 %all-gather.5.cloned.1.call-done = bf16[256,4096]{1,0:T(8,128)(2,1)} async-done(((bf16[256,1024]{1,0:T(8,128)(2,1)}), bf16[256,4096]{1,0:T(8,128)(2,1)}) %all-gather.5.cloned.1.call-update) | async-done | bytes 2097168 | tf_op jit(solution)/shard_map/all_gather | solution.py:30
  58.0 7.8 %fusion.17 = (f32[1024]{0:T(1024)}, bf16[256,1024]{1,0:T(8,128)(2,1)}, bf16[256,1024]{1,0:T(8,128)(2,1)S(1)}) fusion(bf16[256,1024]{1,0:T(8,128)(2,1)} %param.16, f32[256,1024]{1,0:T(8,128)S(1)} %copy.72, bf16[256,4096]{1,0:T(8,128)(2,1)} %all-gather.5.cloned.1.call-done, bf16[1024,4096]{1,0:T(8,128)(2,1)} %param.24), kind=kOutput, calls=%fused_computation.36 | convolution fusion | flops 2149317632 | bytes 13111296 | tf_op jit(solution)/shard_map/dot_general | solution.py:29
  66.0 1.1 fusion.22
  68.9 13.9 %all-reduce = f32[128]{0:T(128)S(1)} all-reduce(f32[128]{0:T(128)S(1)} %dynamic-update-slice.3), channel_id=2, replica_groups=mesh['seq'=8,'head'=4] {'seq'}, use_global_device_ids=true, to_apply=%add | all-reduce | flops 128 | bytes 1024
  84.1 2.0 fusion.10
  86.1 16.6 %all-gather.7.cloned.1.call-done = f32[128,64,128]{2,1,0:T(8,128)} async-done(((f32[16,64,128]{2,1,0:T(8,128)}), f32[128,64,128]{2,1,0:T(8,128)}) %all-gather.7.cloned.1.call-update) | async-done | bytes 4194320 | tf_op jit(solution)/shard_map/all_gather | solution.py:9
  102.8 4.7 %rev.13 = f32[8,16,64,128]{3,2,1,0:T(8,128)} reverse(f32[8,16,64,128]{3,2,1,0:T(8,128)} %bitcast.136), dimensions={0} | reverse | bytes 8388608 | tf_op jit(solution)/shard_map/rev | solution.py:10
  107.5 13.2 %while.15 = (s32[]{:T(128)}, f32[16,64,128]{2,1,0:T(8,128)S(1)}, s32[]{:T(128)}, f32[8,16]{1,0:T(8,128)}, f32[8,16,64,128]{3,2,1,0:T(8,128)}, /*index=5*/s32[]{:T(128)}, s32[]{:T(128)}) while((s32[]{:T(128)}, f32[16,64,128]{2,1,0:T(8,128)S(1)}, s32[]{:T(128)}, f32[8,16]{1,0:T(8,128)}, f32[8,16,64,128]{3,2,1,0:T(8,128)}, ...), condition=%wide.region_3.4_spmd.clone, body=%wide.region_2.3_spmd.clone.sunk | while | flops 524292 | bytes 1573161 | solution.py:20
  108.2 1.2 fusion.62
  110.1 1.2 fusion.62
  112.0 1.2 fusion.62
  113.9 1.2 fusion.62
  115.7 1.2 fusion.62
  117.6 1.2 fusion.62
  119.5 1.2 fusion.62
  120.7 1.2 multiply_reduce_fusion.1
  121.9 7.2 %fusion.1 = bf16[4096,256]{0,1:T(8,128)(2,1)} fusion(bf16[256,1024]{0,1:T(8,128)(2,1)S(1)} %bitcast.142, bf16[4096,1024]{1,0:T(8,128)(2,1)} %param.25), kind=kOutput, calls=%fused_computation.4 | convolution fusion | flops 2148532224 | bytes 11010048 | tf_op jit(solution)/shard_map/dot_general | solution.py:104
  131.0 3.5 %fusion.2 = (f32[16,256]{1,0:T(8,128)S(1)}, f32[16,256]{1,0:T(8,128)S(1)}, bf16[256,256]{1,0:T(8,128)(2,1)S(1)}) fusion(f32[16,256]{1,0:T(8,128)} %copy-done.13, f32[256,256]{1,0:T(8,128)} %copy-done.5, pred[256,256]{1,0:T(8,128)(4,1)} %copy-done.15, bf16[256,16,64]{0,2,1:T(8,128)(2,1)S(1)} %bitcast.135, f32[256,16,64]{0,2,1:T(8,128)S(1)} %bitcast.130, ...), kind=kOutput, calls=%fused_computation.10 | convolution fusion | flops 146202624 | bytes 2097152 | tf_op jit(solution)/shard_map/ihp,jhp->hij/dot_general | solution.py:50
  138.7 13.9 %psum.7 = f32[3,16]{1,0:T(4,128)S(1)} all-reduce(f32[3,16]{1,0:T(4,128)S(1)} %pad_maximum_fusion.1), channel_id=1, replica_groups=mesh['seq'=8,'head'=4] {'seq'}, use_global_device_ids=true, to_apply=%region_20.21 | all-reduce | flops 48 | bytes 384 | tf_op jit(solution)/shard_map/psum | solution.py:113
  153.2 19.8 %reduce-scatter.3.cloned.1.call-done = bf16[1024,256]{0,1:T(8,128)(2,1)} async-done(((bf16[4096,256]{0,1:T(8,128)(2,1)}), bf16[1024,256]{0,1:T(8,128)(2,1)}) %reduce-scatter.3.cloned.1.call-update) | async-done | bytes 524304 | tf_op jit(solution)/shard_map/reduce_scatter | solution.py:103
  173.0 2.0 %copy.78 = bf16[1024,256]{1,0:T(8,128)(2,1)} copy(bf16[1024,256]{0,1:T(8,128)(2,1)} %reduce-scatter.3.cloned.1.call-done) | data formatting | bytes 1048576
  175.0 19.4 %reduce-scatter.5.cloned.1.call-done = bf16[64,256]{1,0:T(8,128)(2,1)} async-done(((bf16[256,256]{1,0:T(8,128)(2,1)}), bf16[64,256]{1,0:T(8,128)(2,1)}) %reduce-scatter.5.cloned.1.call-update) | async-done | bytes 32784 | tf_op jit(solution)/shard_map/reduce_scatter | solution.py:111
  (114 shorter events, 17.3 us)
Async XLA Ops:
  7.2 76.3 %copy-start = (bf16[256,128]{1,0:T(8,128)(2,1)S(1)}, bf16[256,128]{1,0:T(8,128)(2,1)}, u32[]{:S(2)}) copy-start(bf16[256,128]{1,0:T(8,128)(2,1)} %param.17) | copy-start | bytes 196612
  7.2 50.8 %all-gather.5.cloned.1.call-start = ((), (), s32[]{:S(2)}) async-start(), calls=%async_computation.2 | async-start | bytes 2621440 | tf_op jit(solution)/shard_map/all_gather | solution.py:30
  7.9 94.9 %all-gather.7.cloned.1.call-start = ((), (), s32[]{:S(2)}) async-start(), calls=%async_computation.5 | async-start | bytes 4718592 | tf_op jit(solution)/shard_map/all_gather | solution.py:9
  10.8 55.0 %copy-start.16 = (f32[16,2]{0,1:T(2,128)}, f32[16,2]{0,1:T(2,128)S(1)}, u32[]{:S(2)}) copy-start(f32[16,2]{0,1:T(2,128)S(1)} %slice.34) | copy-start | bytes 388
  11.0 54.8 %copy-start.19 = (f32[16]{0:T(128)}, f32[16]{0:T(128)S(1)}, u32[]{:S(2)}) copy-start(f32[16]{0:T(128)S(1)} %get-tuple-element.154) | copy-start | bytes 196
  12.9 53.1 %copy-start.2 = (bf16[256,128]{1,0:T(8,128)(2,1)S(1)}, bf16[256,128]{1,0:T(8,128)(2,1)}, u32[]{:S(2)}) copy-start(bf16[256,128]{1,0:T(8,128)(2,1)} %param.18) | copy-start | bytes 196612
  12.9 54.3 %copy-start.3 = (bf16[256,1024]{1,0:T(8,128)(2,1)S(1)}, bf16[256,1024]{1,0:T(8,128)(2,1)}, u32[]{:S(2)}) copy-start(bf16[256,1024]{1,0:T(8,128)(2,1)} %param.16) | copy-start | bytes 1572868
  67.2 105.8 %reduce-scatter.3.cloned.1.call-start = ((), (), s32[]{:S(2)}) async-start(), calls=%async_computation.3 | async-start | bytes 2621440 | tf_op jit(solution)/shard_map/reduce_scatter | solution.py:103
  84.1 23.4 %copy-start.5 = (f32[256,256]{1,0:T(8,128)}, f32[256,256]{1,0:T(8,128)S(1)}, u32[]{:S(2)}) copy-start(f32[256,256]{1,0:T(8,128)S(1)} %fusion.44) | copy-start | bytes 786436
  107.5 13.2 %copy-start.7 = (f32[256,16]{0,1:T(8,128)S(1)}, f32[256,16]{0,1:T(8,128)}, u32[]{:S(2)}) copy-start(f32[256,16]{0,1:T(8,128)} %get-tuple-element.175) | copy-start | bytes 49156
  107.5 13.2 %copy-start.9 = (f32[256,16]{0,1:T(8,128)S(1)}, f32[256,16]{0,1:T(8,128)}, u32[]{:S(2)}) copy-start(f32[256,16]{0,1:T(8,128)} %get-tuple-element.176) | copy-start | bytes 49156
  107.5 13.2 %copy-start.10 = (f32[256,16]{0,1:T(8,128)S(1)}, f32[256,16]{0,1:T(8,128)}, u32[]{:S(2)}) copy-start(f32[256,16]{0,1:T(8,128)} %get-tuple-element.174) | copy-start | bytes 49156
  107.5 13.2 %copy-start.25 = (f32[16]{0:T(128)S(1)}, f32[16]{0:T(128)}, u32[]{:S(2)}) copy-start(f32[16]{0:T(128)} %param.22) | copy-start | bytes 196
  121.9 7.3 %copy-start.21 = (f32[1024]{0:T(1024)S(1)}, f32[1024]{0:T(1024)}, u32[]{:S(2)}) copy-start(f32[1024]{0:T(1024)} %get-tuple-element.169) | copy-start | bytes 12292
  121.9 8.1 %copy-start.4 = (bf16[256,1024]{1,0:T(8,128)(2,1)S(1)}, bf16[256,1024]{1,0:T(8,128)(2,1)}, u32[]{:S(2)}) copy-start(bf16[256,1024]{1,0:T(8,128)(2,1)} %get-tuple-element.170) | copy-start | bytes 1572868
  121.9 8.3 %copy-start.1 = (bf16[1,1024,128]{2,1,0:T(8,128)(2,1)S(1)}, bf16[1,1024,128]{2,1,0:T(8,128)(2,1)}, u32[]{:S(2)}) copy-start(bf16[1,1024,128]{2,1,0:T(8,128)(2,1)} %param.23) | copy-start | bytes 786436
  129.2 65.2 %reduce-scatter.5.cloned.1.call-start = ((), (), s32[]{:S(2)}) async-start(), calls=%async_computation.4 | async-start | bytes 163840 | tf_op jit(solution)/shard_map/reduce_scatter | solution.py:111
  130.8 3.8 %copy-start.6 = (f32[16,256]{1,0:T(8,128)S(1)}, f32[16,256]{1,0:T(8,128)}, u32[]{:S(2)}) copy-start(f32[16,256]{1,0:T(8,128)} %param.19) | copy-start | bytes 49156
  130.9 3.8 %copy-start.11 = (f32[256,16]{0,1:T(8,128)S(1)}, f32[256,16]{0,1:T(8,128)}, u32[]{:S(2)}) copy-start(f32[256,16]{0,1:T(8,128)} %get-tuple-element.152) | copy-start | bytes 49156
  130.9 4.4 %copy-start.14 = (f32[16,256]{1,0:T(8,128)S(1)}, f32[16,256]{1,0:T(8,128)}, u32[]{:S(2)}) copy-start(f32[16,256]{1,0:T(8,128)} %copy-done.13) | copy-start | bytes 49156
  130.9 5.8 %copy-start.8 = (f32[256,16]{0,1:T(8,128)S(1)}, f32[256,16]{0,1:T(8,128)}, u32[]{:S(2)}) copy-start(f32[256,16]{0,1:T(8,128)} %get-tuple-element.175) | copy-start | bytes 49156
  130.9 6.9 %copy-start.12 = (f32[256,16]{0,1:T(8,128)S(1)}, f32[256,16]{0,1:T(8,128)}, u32[]{:S(2)}) copy-start(f32[256,16]{0,1:T(8,128)} %get-tuple-element.153) | copy-start | bytes 49156
  130.9 6.9 %copy-start.23 = (f32[16]{0:T(128)S(1)}, f32[16]{0:T(128)}, u32[]{:S(2)}) copy-start(f32[16]{0:T(128)} %copy-done.22) | copy-start | bytes 196
  130.9 7.7 %copy-start.24 = (f32[16]{0:T(128)S(1)}, f32[16]{0:T(128)}, u32[]{:S(2)}) copy-start(f32[16]{0:T(128)} %reduce_sum.127) | copy-start | bytes 196
  (7 other events, 15.9 us)
Sparse Core Ops, SparseCore 0:
  9.6 48.3 all-gather.4
  67.3 35.4 all-gather.6
  129.3 43.6 reduce-scatter.2
  175.7 18.6 reduce-scatter.4
where the time goes:
time: 202 us; the launch traced here: 201 us
  waiting for transfers between devices  102 us (50%)
  blocking collectives  27.8 us (14%)
  matrix products  24.4 us (12%)
  local copies, waits for them, and re-layouts  16.4 us (8%)
  other arithmetic  15.7 us (8%)
  between operations  14.7 us (7%)
    all_gather x1, waiting for transfers between devices, shards(): lax.all_gather(out_grad, 'head', axis=1, tiled=True)  45.1 us
    reduce_scatter x1, waiting for transfers between devices, shards(): lax.psum_scatter(lax.dot_general(w_in, x_grad, contract_last, preferred_e...  19.8 us
    reduce_scatter x1, waiting for transfers between devices, shards(): lax.psum_scatter(bc_part.astype(jnp.bfloat16), 'head', scatter_dimension=...  19.4 us
    all_gather x1, waiting for transfers between devices, entering(): pieces = jax.tree.map(lambda part: lax.all_gather(part, axis), value)  16.6 us
    unnamed x1, blocking collectives  13.9 us
    psum x1, blocking collectives, shards(): param_grad = lax.psum(param_terms, 'seq') * norm_scale  13.9 us
    select_n x7, other arithmetic, turn(): jnp.where(position < mine, new, old)  8.18 us
    dot_general x1, matrix products, shards(): lax.dot_general(lax.all_gather(out_grad, 'head', axis=1, tiled=True), w_o...  7.83 us
  transfers between devices with their start and end apart: 4, of which 4 were waited for; matrix products, arithmetic and copies ran while one was open for 10% of the time, Pallas kernels for 0%

commit v1 on v0

--- a/solution.py
+++ b/solution.py
@@ -2,6 +2,14 @@
 import jax.numpy as jnp
 from jax import lax
 from jax.sharding import PartitionSpec as P
+
+
+def gather_by_exchange(array, axis, dim):
+    peers = lax.axis_size(axis)
+    repeats = [peers if d == dim else 1 for d in range(array.ndim)]
+    return lax.all_to_all(
+        jnp.tile(array, repeats), axis, split_axis=dim, concat_axis=dim, tiled=True
+    )
 
 
 def entering(value, axis, join, neutral):
@@ -27,7 +35,7 @@
     state_dim = b_in.shape[1]
     contract_last = (((1,), (1,)), ((), ()))
     head_sum = lax.dot_general(
-        lax.all_gather(out_grad, "head", axis=1, tiled=True),
+        gather_by_exchange(out_grad, "head", 1),
         w_out,
         contract_last,
         preferred_element_type=jnp.float32,

time: 202 us -> 212 us (1.050)
  local copies, waits for them, and re-layouts: 16.4 us -> 23.2 us
  starting transfers between devices: 0.16 us -> 6.61 us
    all_gather x1 -> x0, waiting for transfers between devices: 45.1 us -> none  [shards(): lax.all_gather(out_grad, 'head', axis=1, tiled=True)]
    all_to_all x0 -> x1, waiting for transfers between devices: none -> 44.9 us  [gather_by_exchange(): lax.all_to_all(jnp.tile(array, repeats), axis, split_axis=dim, concat_axi...]
    all_to_all x0 -> x1, starting transfers between devices: none -> 6.35 us  [gather_by_exchange(): lax.all_to_all(jnp.tile(array, repeats), axis, split_axis=dim, concat_axi...]
    another operation x5 -> x6, local copies, waits for them, and re-layouts: 0.33 us -> 3.04 us  [the longest x1 2.7 us: gather_by_exchange(): jnp.tile(array, repeats)]
    all_to_all x0 -> x1, local copies, waits for them, and re-layouts: none -> 2.59 us  [gather_by_exchange(): lax.all_to_all(jnp.tile(array, repeats), axis, split_axis=dim, concat_axi...]
  transfers between devices with their start and end apart: 4 -> 4, of which waited for: 4 -> 4; matrix products, arithmetic and copies ran while one was open for 10% -> 9% of each run, Pallas kernels for 0% -> 0%
where the time goes in v1:
time: 212 us; the launch traced here: 210 us
  waiting for transfers between devices  101 us (48%)
  blocking collectives  27.3 us (13%)
  matrix products  24.5 us (12%)
  local copies, waits for them, and re-layouts  23.2 us (11%)
  between operations  14.7 us (7%)
  other arithmetic  13.6 us (6%)
  starting transfers between devices  6.61 us (3%)
    all_to_all x1, waiting for transfers between devices, gather_by_exchange(): lax.all_to_all(jnp.tile(array, repeats), axis, split_axis=dim, concat_axi...  44.9 us
    reduce_scatter x1, waiting for transfers between devices, shards(): lax.psum_scatter(lax.dot_general(w_in, x_grad, contract_last, preferred_e...  19.6 us
    reduce_scatter x1, waiting for transfers between devices, shards(): lax.psum_scatter(bc_part.astype(jnp.bfloat16), 'head', scatter_dimension=...  19.5 us
    all_gather x1, waiting for transfers between devices, entering(): pieces = jax.tree.map(lambda part: lax.all_gather(part, axis), value)  16.5 us
    psum x1, blocking collectives, shards(): param_grad = lax.psum(param_terms, 'seq') * norm_scale  13.9 us
    unnamed x1, blocking collectives  13.4 us
    select_n x7, other arithmetic, turn(): jnp.where(position < mine, new, old)  8.18 us
    dot_general x1, matrix products, shards(): lax.dot_general(gather_by_exchange(out_grad, 'head', 1), w_out, contract_...  7.92 us
  transfers between devices with their start and end apart: 4, of which 4 were waited for; matrix products, arithmetic and copies ran while one was open for 9% of the time, Pallas kernels for 0%

profile of v1, /device:TPU:0, one launch (start us, length us, event | category | flops | bytes accessed | tf_op | source)
XLA Modules:
  0.0 210.5 jit_solution(15616492040628268656)
XLA Ops:
  7.2 2.7 %tile.2 = bf16[256,4,1024]{2,0,1:T(8,128)(2,1)} broadcast(bf16[256,1024]{1,0:T(8,128)(2,1)} %param.15), dimensions={0,2} | broadcast | bytes 2621440 | tf_op jit(solution)/shard_map/tile | solution.py:11
  9.9 6.3 %all-to-all-start = ((bf16[256,4,1024]{2,0,1:T(8,128)(2,1)}), bf16[256,4,1024]{2,0,1:T(8,128)(2,1)S(1)}, u32[]{:S(2)}, u32[]{:S(2)}) async-start(bf16[256,4,1024]{2,0,1:T(8,128)(2,1)} %tile.2), calls=%async_computation | async-start | bytes 4194304 | tf_op jit(solution)/shard_map/all_to_all | solution.py:10
  18.3 1.3 copy.85
  19.6 44.9 %all-to-all-done = bf16[256,4,1024]{2,0,1:T(8,128)(2,1)S(1)} async-done(((bf16[256,4,1024]{2,0,1:T(8,128)(2,1)}), bf16[256,4,1024]{2,0,1:T(8,128)(2,1)S(1)}, u32[]{:S(2)}, u32[]{:S(2)}) %all-to-all-start) | async-done | bytes 2097184 | tf_op jit(solution)/shard_map/all_to_all | solution.py:10
  64.5 2.6 %copy.80 = bf16[256,4,1024]{0,2,1:T(8,128)(2,1)} copy(bf16[256,4,1024]{2,0,1:T(8,128)(2,1)S(1)} %all-to-all-done) | data formatting | bytes 4194304 | tf_op jit(solution)/shard_map/all_to_all | solution.py:10
  67.1 7.9 %fusion.17 = (f32[1024]{0:T(1024)}, bf16[256,1024]{1,0:T(8,128)(2,1)}, bf16[256,1024]{1,0:T(8,128)(2,1)S(1)}) fusion(bf16[256,1024]{1,0:T(8,128)(2,1)} %param.16, f32[256,1024]{1,0:T(8,128)S(1)} %copy-done.1, bf16[256,4096]{0,1:T(8,128)(2,1)} %bitcast.140, bf16[1024,4096]{1,0:T(8,128)(2,1)} %param.24), kind=kOutput, calls=%fused_computation.36 | convolution fusion | flops 2149317632 | bytes 13111296 | tf_op jit(solution)/shard_map/dot_general | solution.py:37
  76.4 1.2 copy.84
  79.0 13.4 %all-reduce = f32[128]{0:T(128)S(1)} all-reduce(f32[128]{0:T(128)S(1)} %dynamic-update-slice.3), channel_id=2, replica_groups=mesh['seq'=8,'head'=4] {'seq'}, use_global_device_ids=true, to_apply=%add | all-reduce | flops 128 | bytes 1024
  93.8 2.0 fusion.10
  95.8 16.5 %all-gather.4.cloned.1.call-done = f32[128,64,128]{2,1,0:T(8,128)} async-done(((f32[16,64,128]{2,1,0:T(8,128)}), f32[128,64,128]{2,1,0:T(8,128)}) %all-gather.4.cloned.1.call-update) | async-done | bytes 4194320 | tf_op jit(solution)/shard_map/all_gather | solution.py:17
  112.2 4.7 %rev.13 = f32[8,16,64,128]{3,2,1,0:T(8,128)} reverse(f32[8,16,64,128]{3,2,1,0:T(8,128)} %bitcast.137), dimensions={0} | reverse | bytes 8388608 | tf_op jit(solution)/shard_map/rev | solution.py:18
  117.0 13.2 %while.15 = (s32[]{:T(128)}, f32[16,64,128]{2,1,0:T(8,128)S(1)}, s32[]{:T(128)}, f32[8,16]{1,0:T(8,128)}, f32[8,16,64,128]{3,2,1,0:T(8,128)}, /*index=5*/s32[]{:T(128)}, s32[]{:T(128)}) while((s32[]{:T(128)}, f32[16,64,128]{2,1,0:T(8,128)S(1)}, s32[]{:T(128)}, f32[8,16]{1,0:T(8,128)}, f32[8,16,64,128]{3,2,1,0:T(8,128)}, ...), condition=%wide.region_3.4_spmd.clone, body=%wide.region_2.3_spmd.clone.sunk | while | flops 524292 | bytes 1573161 | solution.py:28
  117.7 1.2 fusion.62
  119.6 1.2 fusion.62
  121.4 1.2 fusion.62
  123.3 1.2 fusion.62
  125.2 1.2 fusion.62
  130.2 1.2 multiply_reduce_fusion.1
  131.4 7.2 %fusion.1 = bf16[4096,256]{0,1:T(8,128)(2,1)} fusion(bf16[256,1024]{0,1:T(8,128)(2,1)S(1)} %bitcast.144, bf16[4096,1024]{1,0:T(8,128)(2,1)} %param.25), kind=kOutput, calls=%fused_computation.4 | convolution fusion | flops 2148532224 | bytes 11010048 | tf_op jit(solution)/shard_map/dot_general | solution.py:112
  140.6 3.5 %fusion.2 = (f32[16,256]{1,0:T(8,128)S(1)}, f32[16,256]{1,0:T(8,128)S(1)}, bf16[256,256]{1,0:T(8,128)(2,1)S(1)}) fusion(f32[16,256]{1,0:T(8,128)} %copy-done.14, f32[256,256]{1,0:T(8,128)} %copy-done.5, pred[256,256]{1,0:T(8,128)(4,1)} %copy-done.16, bf16[256,16,64]{0,2,1:T(8,128)(2,1)S(1)} %bitcast.136, f32[256,16,64]{0,2,1:T(8,128)S(1)} %bitcast.131, ...), kind=kOutput, calls=%fused_computation.10 | convolution fusion | flops 146202624 | bytes 2097152 | tf_op jit(solution)/shard_map/ihp,jhp->hij/dot_general | solution.py:58
  148.3 13.9 %psum.7 = f32[3,16]{1,0:T(4,128)S(1)} all-reduce(f32[3,16]{1,0:T(4,128)S(1)} %pad_maximum_fusion.1), channel_id=1, replica_groups=mesh['seq'=8,'head'=4] {'seq'}, use_global_device_ids=true, to_apply=%region_20.21 | all-reduce | flops 48 | bytes 384 | tf_op jit(solution)/shard_map/psum | solution.py:121
  162.8 19.6 %reduce-scatter.3.cloned.1.call-done = bf16[1024,256]{0,1:T(8,128)(2,1)} async-done(((bf16[4096,256]{0,1:T(8,128)(2,1)}), bf16[1024,256]{0,1:T(8,128)(2,1)}) %reduce-scatter.3.cloned.1.call-update) | async-done | bytes 524304 | tf_op jit(solution)/shard_map/reduce_scatter | solution.py:111
  182.5 2.0 copy.91
  184.5 19.5 %reduce-scatter.5.cloned.1.call-done = bf16[64,256]{1,0:T(8,128)(2,1)} async-done(((bf16[256,256]{1,0:T(8,128)(2,1)}), bf16[64,256]{1,0:T(8,128)(2,1)}) %reduce-scatter.5.cloned.1.call-update) | async-done | bytes 32784 | tf_op jit(solution)/shard_map/reduce_scatter | solution.py:119
  (121 shorter events, 19.2 us)
Async XLA Ops:
  7.2 86.0 %copy-start = (bf16[256,128]{1,0:T(8,128)(2,1)S(1)}, bf16[256,128]{1,0:T(8,128)(2,1)}, u32[]{:S(2)}) copy-start(bf16[256,128]{1,0:T(8,128)(2,1)} %param.17) | copy-start | bytes 196612
  7.2 9.1 %copy-start.28 = (f32[16]{0:T(128)S(1)}, f32[16]{0:T(128)}, u32[]{:S(2)}) copy-start(f32[16]{0:T(128)} %param.21) | copy-start | bytes 196
  7.2 9.1 %copy-start.6 = (f32[16,256]{1,0:T(8,128)S(1)}, f32[16,256]{1,0:T(8,128)}, u32[]{:S(2)}) copy-start(f32[16,256]{1,0:T(8,128)} %param.19) | copy-start | bytes 49156
  7.2 9.1 %copy-start.19 = (f32[16]{0:T(128)S(1)}, f32[16]{0:T(128)}, u32[]{:S(2)}) copy-start(f32[16]{0:T(128)} %param.20) | copy-start | bytes 196
  9.9 54.5 %all-to-all-start = ((bf16[256,4,1024]{2,0,1:T(8,128)(2,1)}), bf16[256,4,1024]{2,0,1:T(8,128)(2,1)S(1)}, u32[]{:S(2)}, u32[]{:S(2)}) async-start(bf16[256,4,1024]{2,0,1:T(8,128)(2,1)} %tile.2), calls=%async_computation | async-start | bytes 4194304 | tf_op jit(solution)/shard_map/all_to_all | solution.py:10
  16.3 96.0 %all-gather.4.cloned.1.call-start = ((), (), s32[]{:S(2)}) async-start(), calls=%async_computation.5 | async-start | bytes 4718592 | tf_op jit(solution)/shard_map/all_gather | solution.py:17
  17.2 57.8 %copy-start.17 = (f32[16,2]{0,1:T(2,128)}, f32[16,2]{0,1:T(2,128)S(1)}, u32[]{:S(2)}) copy-start(f32[16,2]{0,1:T(2,128)S(1)} %slice.34) | copy-start | bytes 388
  17.5 57.5 %copy-start.21 = (f32[16]{0:T(128)}, f32[16]{0:T(128)S(1)}, u32[]{:S(2)}) copy-start(f32[16]{0:T(128)S(1)} %get-tuple-element.158) | copy-start | bytes 196
  19.6 47.5 %copy-start.1 = (f32[256,1024]{1,0:T(8,128)S(1)}, f32[256,1024]{1,0:T(8,128)}, u32[]{:S(2)}) copy-start(f32[256,1024]{1,0:T(8,128)} %copy.85) | copy-start | bytes 3145732
  67.1 8.1 %copy-start.3 = (bf16[256,128]{1,0:T(8,128)(2,1)S(1)}, bf16[256,128]{1,0:T(8,128)(2,1)}, u32[]{:S(2)}) copy-start(bf16[256,128]{1,0:T(8,128)(2,1)} %param.18) | copy-start | bytes 196612
  76.3 106.1 %reduce-scatter.3.cloned.1.call-start = ((), (), s32[]{:S(2)}) async-start(), calls=%async_computation.3 | async-start | bytes 2621440 | tf_op jit(solution)/shard_map/reduce_scatter | solution.py:111
  93.7 23.2 %copy-start.5 = (f32[256,256]{1,0:T(8,128)}, f32[256,256]{1,0:T(8,128)S(1)}, u32[]{:S(2)}) copy-start(f32[256,256]{1,0:T(8,128)S(1)} %fusion.44) | copy-start | bytes 786436
  116.9 13.2 %copy-start.8 = (f32[256,16]{0,1:T(8,128)S(1)}, f32[256,16]{0,1:T(8,128)}, u32[]{:S(2)}) copy-start(f32[256,16]{0,1:T(8,128)} %get-tuple-element.179) | copy-start | bytes 49156
  116.9 13.2 %copy-start.10 = (f32[256,16]{0,1:T(8,128)S(1)}, f32[256,16]{0,1:T(8,128)}, u32[]{:S(2)}) copy-start(f32[256,16]{0,1:T(8,128)} %get-tuple-element.180) | copy-start | bytes 49156
  117.0 13.2 %copy-start.11 = (f32[256,16]{0,1:T(8,128)S(1)}, f32[256,16]{0,1:T(8,128)}, u32[]{:S(2)}) copy-start(f32[256,16]{0,1:T(8,128)} %get-tuple-element.178) | copy-start | bytes 49156
  117.0 13.2 %copy-start.27 = (f32[16]{0:T(128)S(1)}, f32[16]{0:T(128)}, u32[]{:S(2)}) copy-start(f32[16]{0:T(128)} %param.22) | copy-start | bytes 196
  131.4 7.5 %copy-start.23 = (f32[1024]{0:T(1024)S(1)}, f32[1024]{0:T(1024)}, u32[]{:S(2)}) copy-start(f32[1024]{0:T(1024)} %get-tuple-element.173) | copy-start | bytes 12292
  131.4 8.3 %copy-start.4 = (bf16[256,1024]{1,0:T(8,128)(2,1)S(1)}, bf16[256,1024]{1,0:T(8,128)(2,1)}, u32[]{:S(2)}) copy-start(bf16[256,1024]{1,0:T(8,128)(2,1)} %get-tuple-element.174) | copy-start | bytes 1572868
  131.4 8.5 %copy-start.2 = (bf16[1,1024,128]{2,1,0:T(8,128)(2,1)S(1)}, bf16[1,1024,128]{2,1,0:T(8,128)(2,1)}, u32[]{:S(2)}) copy-start(bf16[1,1024,128]{2,1,0:T(8,128)(2,1)} %param.23) | copy-start | bytes 786436
  138.7 65.3 %reduce-scatter.5.cloned.1.call-start = ((), (), s32[]{:S(2)}) async-start(), calls=%async_computation.4 | async-start | bytes 163840 | tf_op jit(solution)/shard_map/reduce_scatter | solution.py:119
  140.6 5.8 %copy-start.9 = (f32[256,16]{0,1:T(8,128)S(1)}, f32[256,16]{0,1:T(8,128)}, u32[]{:S(2)}) copy-start(f32[256,16]{0,1:T(8,128)} %get-tuple-element.179) | copy-start | bytes 49156
  140.6 6.9 %copy-start.13 = (f32[256,16]{0,1:T(8,128)S(1)}, f32[256,16]{0,1:T(8,128)}, u32[]{:S(2)}) copy-start(f32[256,16]{0,1:T(8,128)} %get-tuple-element.157) | copy-start | bytes 49156
  140.6 6.9 %copy-start.25 = (f32[16]{0:T(128)S(1)}, f32[16]{0:T(128)}, u32[]{:S(2)}) copy-start(f32[16]{0:T(128)} %copy-done.24) | copy-start | bytes 196
  140.6 7.7 %copy-start.26 = (f32[16]{0:T(128)S(1)}, f32[16]{0:T(128)}, u32[]{:S(2)}) copy-start(f32[16]{0:T(128)} %reduce_sum.127) | copy-start | bytes 196
  (10 other events, 29.7 us)
Sparse Core Ops, SparseCore 0:
  76.4 35.7 all-gather.3
  138.8 43.6 reduce-scatter.2
  185.3 18.6 reduce-scatter.4
